TPU v7x, 32 devices: a whole 2x2x4 slice. The times are simulated.
32 devices in a mesh: wide: 8 (over y, x, core), narrow: 4 (over z).
Axes of the slice: x: 2, y: 2, z: 4, core: 2. Of those that a mesh axis runs over, the one named last changes fastest.
Arguments:
- amplitudes: float32 [2, 8, 8, 4, 128, 128], P(None, None, 'wide', 'narrow'), may hold values from -6 to 6
- gates: float32 [3, 2, 2, 128, 128], replicated, may hold values from -0.375 to 0.375
Outputs:
- final_state: float32 [2, 8, 8, 4, 128, 128], P(None, None, 'wide', 'narrow')
All inputs are finite; a program needn't handle non-finite values.
Results may differ from a plain program's by a relative error of at most 0.0001.
Values sent between devices are 32-bit elements; how exact they have to be, the bound alone decides.
A program may use at most 64 MiB of HBM per device.

v0:
```python
import jax
import jax.numpy as jnp
from jax import lax
from jax.sharding import PartitionSpec as P

precise = lax.Precision.HIGHEST


def blocks(matrix):
    return jnp.stack([jnp.stack([matrix[0], -matrix[1]]), jnp.stack([matrix[1], matrix[0]])])


def on_rows(vector, matrix):
    return jnp.einsum("cdjk,drkb->crjb", blocks(matrix), vector, precision=precise)


def on_columns(vector, matrix):
    return jnp.einsum("cdjk,drak->craj", blocks(matrix), vector, precision=precise)


def shards(amplitudes, gates):
    layout = amplitudes.shape
    slab_count = layout[1]
    gate_order = layout[4]
    vector = amplitudes.reshape(2, slab_count, gate_order, gate_order)
    vector = on_rows(vector, gates[0, 0])
    vector = on_columns(vector, gates[0, 1])
    resident = vector.reshape(layout)
    arrived = lax.all_to_all(resident, "wide", split_axis=4, concat_axis=2, tiled=True)
    items_here = arrived.shape[1]
    slab_data = arrived.reshape(2, items_here, gate_order, gate_order)
    slab_data = on_rows(slab_data, gates[1, 0])
    slab_data = on_columns(slab_data, gates[1, 1])
    resident = slab_data.reshape(2, items_here, 1, 1, gate_order, gate_order)
    arrived = lax.all_to_all(resident, "narrow", split_axis=4, concat_axis=3, tiled=True)
    vector = arrived.reshape(2, slab_count, gate_order, gate_order)
    vector = on_rows(vector, gates[2, 0])
    vector = on_columns(vector, gates[2, 1])
    return vector.reshape(layout)


def solution(mesh):
    return jax.shard_map(
        shards,
        mesh=mesh,
        in_specs=(P(None, None, "wide", "narrow", None, None), P()),
        out_specs=P(None, None, "wide", "narrow", None, None),
        check_vma=False,
    )
```

profile of v0, /device:TPU:2, one launch (start us, length us, event | category | flops | bytes accessed | tf_op | source)
XLA Modules:
  0.0 62.3 jit_solution(2130488809126210702)
XLA Ops:
  0.0 0.0 copy-start
  0.0 0.0 copy-start.1
  0.0 1.3 %slice_bitcast_fusion = (f32[1,128,128]{2,1,0:T(8,128)S(1)}, f32[1,128,128]{2,1,0:T(8,128)S(1)}, f32[1,128,128]{2,1,0:T(8,128)S(1)}, f32[1,128,128]{2,1,0:T(8,12...) fusion(f32[3,2,2,128,128]{4,3,2,1,0:T(8,128)} %param.3), kind=kLoop, calls=%fused_computation.39 | loop fusion | bytes 1572864 | tf_op jit(solution)/shard_map/squeeze | solution.py:10
  1.3 0.2 copy-done.1
  1.6 0.2 copy-done
  1.8 1.0 %convolution_bitcast_fusion.5 = f32[2,8,128,128,1]{3,2,0,4,1:T(8,128)S(1)} fusion(f32[1,2,128,128]{3,2,1,0:T(8,128)S(1)} %get-tuple-element.34, f32[1,2,128,128]{3,2,1,0:T(8,128)S(1)} %get-tuple-element.33, f32[2,8,1,1,128,128]{5,4,3,2,1,0:T(8,128)S(1)} %copy-done), kind=kOutput, calls=%fused_computation.5 | convolution fusion | flops 805371904 | bytes 2359296 | tf_op jit(solution)/shard_map/cdjk,drkb->crjb/dot_general | solution.py:14
  2.8 1.0 %convolution_bitcast_fusion.4 = f32[2,8,1,1,128,128]{5,4,0,1,3,2:T(8,128)S(1)} fusion(f32[2,8,128,128,1]{3,2,0,4,1:T(8,128)S(1)} %convolution_bitcast_fusion.5, f32[1,2,128,128]{3,2,1,0:T(8,128)S(1)} %get-tuple-element.35, f32[1,2,128,128]{3,2,1,0:T(8,128)S(1)} %get-tuple-element.36), kind=kOutput, calls=%fused_computation.4 | convolution fusion | flops 805371904 | bytes 2359296 | tf_op jit(solution)/shard_map/cdjk,drak->craj/dot_general | solution.py:18
  3.9 1.8 %copy.4 = f32[2,8,1,1,128,128]{5,0,1,3,2,4:T(2,128)} copy(f32[2,8,1,1,128,128]{5,4,0,1,3,2:T(8,128)S(1)} %convolution_bitcast_fusion.4) | data formatting | bytes 2097152 | tf_op jit(solution)/shard_map/reshape | solution.py:28
  5.6 4.2 %all-to-all-start = ((f32[2,8,1,1,128,128]{5,0,1,3,2,4:T(2,128)}), f32[2,8,1,1,128,128]{5,0,1,3,2,4:T(2,128)S(1)}, u32[]{:S(2)}, u32[]{:S(2)}) async-start(f32[2,8,1,1,128,128]{5,0,1,3,2,4:T(2,128)} %copy.4), calls=%async_computation | async-start | bytes 2097152 | tf_op jit(solution)/shard_map/all_to_all | solution.py:29
  9.9 13.8 %all-to-all-done = f32[2,8,1,1,128,128]{5,0,1,3,2,4:T(2,128)S(1)} async-done(((f32[2,8,1,1,128,128]{5,0,1,3,2,4:T(2,128)}), f32[2,8,1,1,128,128]{5,0,1,3,2,4:T(2,128)S(1)}, u32[]{:S(2)}, u32[]{:S(2)}) %all-to-all-start) | async-done | bytes 1048608 | tf_op jit(solution)/shard_map/all_to_all | solution.py:29
  23.8 1.4 %convolution_bitcast_fusion.3 = f32[2,8,128,128,1]{3,2,0,4,1:T(8,128)S(1)} fusion(f32[2,8,128,128,1]{3,0,1,2,4:T(2,128)S(1)} %bitcast.142, f32[1,2,128,128]{3,2,1,0:T(8,128)S(1)} %get-tuple-element.30, f32[1,2,128,128]{3,2,1,0:T(8,128)S(1)} %get-tuple-element.29), kind=kOutput, calls=%fused_computation.3 | convolution fusion | flops 805371904 | bytes 2359296 | tf_op jit(solution)/shard_map/cdjk,drkb->crjb/dot_general | solution.py:14
  25.2 1.0 %convolution_bitcast_fusion.2 = f32[2,8,1,1,128,128]{5,4,0,1,3,2:T(8,128)S(1)} fusion(f32[2,8,128,128,1]{3,2,0,4,1:T(8,128)S(1)} %convolution_bitcast_fusion.3, f32[1,2,128,128]{3,2,1,0:T(8,128)S(1)} %get-tuple-element.37, f32[1,2,128,128]{3,2,1,0:T(8,128)S(1)} %get-tuple-element.38), kind=kOutput, calls=%fused_computation.2 | convolution fusion | flops 805371904 | bytes 2359296 | tf_op jit(solution)/shard_map/cdjk,drak->craj/dot_general | solution.py:18
  26.2 1.8 %copy.5 = f32[2,8,1,1,128,128]{5,0,1,3,2,4:T(2,128)} copy(f32[2,8,1,1,128,128]{5,4,0,1,3,2:T(8,128)S(1)} %convolution_bitcast_fusion.2) | data formatting | bytes 2097152 | tf_op jit(solution)/shard_map/reshape | solution.py:34
  28.0 4.9 %all-to-all-start.1 = ((f32[2,8,1,1,128,128]{5,0,1,3,2,4:T(2,128)}), f32[2,8,1,1,128,128]{5,0,1,3,2,4:T(2,128)S(1)}, u32[]{:S(2)}, u32[]{:S(2)}) async-start(f32[2,8,1,1,128,128]{5,0,1,3,2,4:T(2,128)} %copy.5), calls=%async_computation.1 | async-start | bytes 2097152 | tf_op jit(solution)/shard_map/all_to_all | solution.py:35
  32.9 25.9 %all-to-all-done.1 = f32[2,8,1,1,128,128]{5,0,1,3,2,4:T(2,128)S(1)} async-done(((f32[2,8,1,1,128,128]{5,0,1,3,2,4:T(2,128)}), f32[2,8,1,1,128,128]{5,0,1,3,2,4:T(2,128)S(1)}, u32[]{:S(2)}, u32[]{:S(2)}) %all-to-all-start.1) | async-done | bytes 1048608 | tf_op jit(solution)/shard_map/all_to_all | solution.py:35
  58.8 1.4 %convolution_bitcast_fusion.1 = f32[2,8,128,128,1]{3,2,0,4,1:T(8,128)S(1)} fusion(f32[2,8,128,128,1]{3,0,1,2,4:T(2,128)S(1)} %bitcast.141, f32[1,2,128,128]{3,2,1,0:T(8,128)S(1)} %get-tuple-element.26, f32[1,2,128,128]{3,2,1,0:T(8,128)S(1)} %get-tuple-element.25), kind=kOutput, calls=%fused_computation.1 | convolution fusion | flops 805371904 | bytes 2359296 | tf_op jit(solution)/shard_map/cdjk,drkb->crjb/dot_general | solution.py:14
  60.2 1.0 %convolution_bitcast_fusion = f32[2,8,1,1,128,128]{5,4,0,1,3,2:T(8,128)S(1)} fusion(f32[2,8,128,128,1]{3,2,0,4,1:T(8,128)S(1)} %convolution_bitcast_fusion.1, f32[1,2,128,128]{3,2,1,0:T(8,128)S(1)} %get-tuple-element.39, f32[1,2,128,128]{3,2,1,0:T(8,128)S(1)} %get-tuple-element.40), kind=kOutput, calls=%fused_computation | convolution fusion | flops 805371904 | bytes 2359296 | tf_op jit(solution)/shard_map/cdjk,drak->craj/dot_general | solution.py:18
  61.3 1.1 %copy.6 = f32[2,8,1,1,128,128]{5,4,3,2,1,0:T(8,128)} copy(f32[2,8,1,1,128,128]{5,4,0,1,3,2:T(8,128)S(1)} %convolution_bitcast_fusion) | data formatting | bytes 2097152 | tf_op jit(solution)/shard_map/reshape | solution.py:39
  (4 shorter events, 0.1 us)
Async XLA Ops:
  0.0 1.8 %copy-start = (f32[2,8,1,1,128,128]{5,4,3,2,1,0:T(8,128)S(1)}, f32[2,8,1,1,128,128]{5,4,3,2,1,0:T(8,128)}, u32[]{:S(2)}) copy-start(f32[2,8,1,1,128,128]{5,4,3,2,1,0:T(8,128)} %param.2) | copy-start | bytes 3145732
  0.0 1.5 %copy-start.1 = (f32[3,2,2,128,128]{4,3,2,1,0:T(8,128)S(1)}, f32[3,2,2,128,128]{4,3,2,1,0:T(8,128)}, u32[]{:S(2)}) copy-start(f32[3,2,2,128,128]{4,3,2,1,0:T(8,128)} %param.3) | copy-start | bytes 2359300
  5.6 18.1 %all-to-all-start = ((f32[2,8,1,1,128,128]{5,0,1,3,2,4:T(2,128)}), f32[2,8,1,1,128,128]{5,0,1,3,2,4:T(2,128)S(1)}, u32[]{:S(2)}, u32[]{:S(2)}) async-start(f32[2,8,1,1,128,128]{5,0,1,3,2,4:T(2,128)} %copy.4), calls=%async_computation | async-start | bytes 2097152 | tf_op jit(solution)/shard_map/all_to_all | solution.py:29
  28.0 30.8 %all-to-all-start.1 = ((f32[2,8,1,1,128,128]{5,0,1,3,2,4:T(2,128)}), f32[2,8,1,1,128,128]{5,0,1,3,2,4:T(2,128)S(1)}, u32[]{:S(2)}, u32[]{:S(2)}) async-start(f32[2,8,1,1,128,128]{5,0,1,3,2,4:T(2,128)} %copy.5), calls=%async_computation.1 | async-start | bytes 2097152 | tf_op jit(solution)/shard_map/all_to_all | solution.py:35
where the time goes:
time: 62.6 us; the launch traced here: 62.3 us
  waiting for transfers between devices  39.7 us (63%)
  starting transfers between devices  9.12 us (15%)
  matrix products  6.91 us (11%)
  local copies, waits for them, and re-layouts  6.33 us (10%)
    all_to_all x1, waiting for transfers between devices, shards(): lax.all_to_all(resident, 'narrow', split_axis=4, concat_axis=3, tiled=True)  25.9 us
    all_to_all x1, waiting for transfers between devices, shards(): lax.all_to_all(resident, 'wide', split_axis=4, concat_axis=2, tiled=True)  13.8 us
    all_to_all x1, starting transfers between devices, shards(): lax.all_to_all(resident, 'narrow', split_axis=4, concat_axis=3, tiled=True)  4.87 us
    all_to_all x1, starting transfers between devices, shards(): lax.all_to_all(resident, 'wide', split_axis=4, concat_axis=2, tiled=True)  4.25 us
    dot_general x3, matrix products, on_rows(): jnp.einsum('cdjk,drkb->crjb', blocks(matrix), vector, precision=precise)  3.83 us
    dot_general x3, matrix products, on_columns(): jnp.einsum('cdjk,drak->craj', blocks(matrix), vector, precision=precise)  3.08 us
    reshape x1, local copies, waits for them, and re-layouts, shards(): resident = vector.reshape(layout)  1.78 us
    reshape x1, local copies, waits for them, and re-layouts, shards(): resident = slab_data.reshape(2, items_here, 1, 1, gate_order, gate_order)  1.78 us
  transfers between devices with their start and end apart: 2, of which 2 were waited for; matrix products, arithmetic and copies ran while one was open for 0% of the time, Pallas kernels for 0%

commit v1 on v0

--- a/solution.py
+++ b/solution.py
@@ -26,7 +26,10 @@
     vector = on_rows(vector, gates[0, 0])
     vector = on_columns(vector, gates[0, 1])
     resident = vector.reshape(layout)
-    arrived = lax.all_to_all(resident, "wide", split_axis=4, concat_axis=2, tiled=True)
+    arrived = jnp.concatenate(
+        lax.all_to_all(jnp.stack(jnp.split(resident, lax.axis_size("wide"), axis=4)), "wide", 0, 0),
+        axis=2,
+    )
     items_here = arrived.shape[1]
     slab_data = arrived.reshape(2, items_here, gate_order, gate_order)
     slab_data = on_rows(slab_data, gates[1, 0])

time: 62.6 us -> 69.3 us (1.11)
  local copies, waits for them, and re-layouts: 6.33 us -> 10.5 us
  matrix products: 6.91 us -> 9.42 us
    unnamed x4 -> x11, local copies, waits for them, and re-layouts: 0.37 us -> 5.02 us
    reshape x1, local copies, waits for them, and re-layouts: 1.78 us -> 0.1 us  [shards(): jnp.concatenate(lax.all_to_all(jnp.stack(jnp.split(resident, lax.axis_siz...]
    dot_general x3, matrix products: 3.08 us -> 4.65 us  [on_columns(): jnp.einsum('cdjk,drak->craj', blocks(matrix), vector, precision=precise)]
    dot_general x3, matrix products: 3.83 us -> 4.76 us  [on_rows(): jnp.einsum('cdjk,drkb->crjb', blocks(matrix), vector, precision=precise)]
  transfers between devices with their start and end apart: 2 -> 2, of which waited for: 2 -> 2; matrix products, arithmetic and copies ran while one was open for 0% -> 1% of each run, Pallas kernels for 0% -> 0%
where the time goes in v1:
time: 69.3 us; the launch traced here: 69 us
  waiting for transfers between devices  39.1 us (56%)
  local copies, waits for them, and re-layouts  10.5 us (15%)
  matrix products  9.42 us (14%)
  starting transfers between devices  9.12 us (13%)
  other arithmetic  0.77 us (1%)
    all_to_all x1, waiting for transfers between devices, shards(): lax.all_to_all(resident, 'narrow', split_axis=4, concat_axis=3, tiled=True)  25.3 us
    all_to_all x1, waiting for transfers between devices, shards(): lax.all_to_all(jnp.stack(jnp.split(resident, lax.axis_size('wide'), axis=...  13.8 us
    unnamed x11, local copies, waits for them, and re-layouts  5.02 us
    all_to_all x1, starting transfers between devices, shards(): lax.all_to_all(resident, 'narrow', split_axis=4, concat_axis=3, tiled=True)  4.87 us
    dot_general x3, matrix products, on_rows(): jnp.einsum('cdjk,drkb->crjb', blocks(matrix), vector, precision=precise)  4.76 us
    dot_general x3, matrix products, on_columns(): jnp.einsum('cdjk,drak->craj', blocks(matrix), vector, precision=precise)  4.65 us
    all_to_all x1, starting transfers between devices, shards(): lax.all_to_all(jnp.stack(jnp.split(resident, lax.axis_size('wide'), axis=...  4.25 us
    reshape x1, local copies, waits for them, and re-layouts, shards(): resident = slab_data.reshape(2, items_here, 1, 1, gate_order, gate_order)  1.78 us
  transfers between devices with their start and end apart: 2, of which 2 were waited for; matrix products, arithmetic and copies ran while one was open for 1% of the time, Pallas kernels for 0%

profile of v1, /device:TPU:2, one launch (start us, length us, event | category | flops | bytes accessed | tf_op | source)
XLA Modules:
  0.0 69.0 jit_solution(16860409373474066038)
XLA Ops:
  0.0 0.0 copy-start
  0.0 0.0 copy-start.1
  0.0 1.3 %slice_bitcast_fusion.8 = (f32[1,128,128]{2,1,0:T(8,128)S(1)}, f32[1,128,128]{2,1,0:T(8,128)S(1)}, f32[1,128,128]{2,1,0:T(8,128)S(1)}, f32[1,128,128]{2,1,0:T(8,...) fusion(f32[3,2,2,128,128]{4,3,2,1,0:T(8,128)} %param.3), kind=kLoop, calls=%fused_computation.55 | loop fusion | bytes 1572864 | tf_op jit(solution)/shard_map/squeeze | solution.py:10
  1.3 0.2 copy-done.1
  1.6 0.2 copy-done
  1.8 1.0 %convolution_bitcast_fusion.5 = f32[2,8,128,128,1]{3,2,0,4,1:T(8,128)S(1)} fusion(f32[1,2,128,128]{3,2,1,0:T(8,128)S(1)} %get-tuple-element.34, f32[1,2,128,128]{3,2,1,0:T(8,128)S(1)} %get-tuple-element.33, f32[2,8,1,1,128,128]{5,4,3,2,1,0:T(8,128)S(1)} %copy-done), kind=kOutput, calls=%fused_computation.5 | convolution fusion | flops 805371904 | bytes 2359296 | tf_op jit(solution)/shard_map/cdjk,drkb->crjb/dot_general | solution.py:14
  2.8 1.0 %convolution_bitcast_fusion.4 = f32[2,8,1,1,128,128]{5,4,0,1,3,2:T(8,128)S(1)} fusion(f32[2,8,128,128,1]{3,2,0,4,1:T(8,128)S(1)} %convolution_bitcast_fusion.5, f32[1,2,128,128]{3,2,1,0:T(8,128)S(1)} %get-tuple-element.35, f32[1,2,128,128]{3,2,1,0:T(8,128)S(1)} %get-tuple-element.36), kind=kOutput, calls=%fused_computation.4 | convolution fusion | flops 805371904 | bytes 2359296 | tf_op jit(solution)/shard_map/cdjk,drak->craj/dot_general | solution.py:18
  3.9 0.7 fusion.22
  4.5 0.7 fusion.21
  5.2 0.7 fusion.20
  5.8 0.7 fusion.19
  6.5 0.7 fusion.18
  7.2 0.7 fusion.17
  7.8 0.7 fusion.16
  8.5 0.7 fusion.15
  9.2 4.2 %all-to-all-start = ((f32[8,2,8,1,1,16,128]{6,5,1,2,4,3,0:T(8,128)}), f32[8,2,8,1,1,16,128]{6,5,1,2,4,3,0:T(8,128)S(1)}, u32[]{:S(2)}, u32[]{:S(2)}) async-start(f32[8,2,8,1,1,16,128]{6,5,1,2,4,3,0:T(8,128)} %fusion.15), calls=%async_computation | async-start | bytes 2097152 | tf_op jit(solution)/shard_map/all_to_all | solution.py:30
  13.5 13.8 %all-to-all-done = f32[8,2,8,1,1,16,128]{6,5,1,2,4,3,0:T(8,128)S(1)} async-done(((f32[8,2,8,1,1,16,128]{6,5,1,2,4,3,0:T(8,128)}), f32[8,2,8,1,1,16,128]{6,5,1,2,4,3,0:T(8,128)S(1)}, u32[]{:S(2)}, u32[]{:S(2)}) %all-to-all-start) | async-done | bytes 1048608 | tf_op jit(solution)/shard_map/all_to_all | solution.py:30
  27.3 0.1 copy.7
  27.4 1.8 %convolution_bitcast_fusion.3 = f32[2,8,128,128,1]{2,3,0,4,1:T(8,128)S(1)} fusion(f32[2,8,128,128,1]{3,2,1,0,4:T(8,128)S(1)} %bitcast.179, f32[1,2,128,128]{3,2,1,0:T(8,128)S(1)} %get-tuple-element.30, f32[1,2,128,128]{3,2,1,0:T(8,128)S(1)} %get-tuple-element.29), kind=kOutput, calls=%fused_computation.3 | convolution fusion | flops 805371904 | bytes 2359296 | tf_op jit(solution)/shard_map/cdjk,drkb->crjb/dot_general | solution.py:14
  29.2 1.8 %convolution_bitcast_fusion.2 = f32[2,8,1,1,128,128]{5,4,0,1,3,2:T(8,128)S(1)} fusion(f32[2,8,128,128,1]{2,3,0,4,1:T(8,128)S(1)} %convolution_bitcast_fusion.3, f32[1,2,128,128]{3,2,1,0:T(8,128)S(1)} %get-tuple-element.28, f32[1,2,128,128]{3,2,1,0:T(8,128)S(1)} %get-tuple-element.27), kind=kOutput, calls=%fused_computation.2 | convolution fusion | flops 805371904 | bytes 2359296 | tf_op jit(solution)/shard_map/cdjk,drak->craj/dot_general | solution.py:18
  31.1 1.8 %copy.10 = f32[2,8,1,1,128,128]{5,0,1,3,2,4:T(2,128)} copy(f32[2,8,1,1,128,128]{5,4,0,1,3,2:T(8,128)S(1)} %convolution_bitcast_fusion.2) | data formatting | bytes 2097152 | tf_op jit(solution)/shard_map/reshape | solution.py:37
  32.8 4.9 %all-to-all-start.1 = ((f32[2,8,1,1,128,128]{5,0,1,3,2,4:T(2,128)}), f32[2,8,1,1,128,128]{5,0,1,3,2,4:T(2,128)S(1)}, u32[]{:S(2)}, u32[]{:S(2)}) async-start(f32[2,8,1,1,128,128]{5,0,1,3,2,4:T(2,128)} %copy.10), calls=%async_computation.1 | async-start | bytes 2097152 | tf_op jit(solution)/shard_map/all_to_all | solution.py:38
  37.7 0.7 maximum_bitcast_fusion.20
  38.4 25.3 %all-to-all-done.1 = f32[2,8,1,1,128,128]{5,0,1,3,2,4:T(2,128)S(1)} async-done(((f32[2,8,1,1,128,128]{5,0,1,3,2,4:T(2,128)}), f32[2,8,1,1,128,128]{5,0,1,3,2,4:T(2,128)S(1)}, u32[]{:S(2)}, u32[]{:S(2)}) %all-to-all-start.1) | async-done | bytes 1048608 | tf_op jit(solution)/shard_map/all_to_all | solution.py:38
  63.7 0.5 copy.11
  64.2 1.9 %convolution_bitcast_fusion.1 = f32[2,8,128,128,1]{2,3,0,4,1:T(8,128)S(1)} fusion(f32[2,8,1,1,128,128]{4,5,0,1,3,2:T(8,128)S(1)} %copy.11, f32[1,2,128,128]{3,2,1,0:T(8,128)} %get-tuple-element.26, f32[1,2,128,128]{3,2,1,0:T(8,128)S(1)} %get-tuple-element.25), kind=kOutput, calls=%fused_computation.1 | convolution fusion | flops 805371904 | bytes 2359296 | tf_op jit(solution)/shard_map/cdjk,drkb->crjb/dot_general | solution.py:14
  66.1 1.8 %convolution_bitcast_fusion = f32[2,8,1,1,128,128]{5,4,0,1,3,2:T(8,128)S(1)} fusion(f32[2,8,128,128,1]{2,3,0,4,1:T(8,128)S(1)} %convolution_bitcast_fusion.1, f32[1,2,128,128]{3,2,1,0:T(8,128)S(1)} %get-tuple-element.37, f32[1,2,128,128]{3,2,1,0:T(8,128)S(1)} %get-tuple-element.38), kind=kOutput, calls=%fused_computation | convolution fusion | flops 805371904 | bytes 2359296 | tf_op jit(solution)/shard_map/cdjk,drak->craj/dot_general | solution.py:18
  67.9 1.1 %copy.13 = f32[2,8,1,1,128,128]{5,4,3,2,1,0:T(8,128)} copy(f32[2,8,1,1,128,128]{5,4,0,1,3,2:T(8,128)S(1)} %convolution_bitcast_fusion) | data formatting | bytes 2097152 | tf_op jit(solution)/shard_map/reshape | solution.py:42
  (4 shorter events, 0.1 us)
Async XLA Ops:
  0.0 1.8 %copy-start = (f32[2,8,1,1,128,128]{5,4,3,2,1,0:T(8,128)S(1)}, f32[2,8,1,1,128,128]{5,4,3,2,1,0:T(8,128)}, u32[]{:S(2)}) copy-start(f32[2,8,1,1,128,128]{5,4,3,2,1,0:T(8,128)} %param.2) | copy-start | bytes 3145732
  0.0 1.5 %copy-start.1 = (f32[3,2,2,128,128]{4,3,2,1,0:T(8,128)S(1)}, f32[3,2,2,128,128]{4,3,2,1,0:T(8,128)}, u32[]{:S(2)}) copy-start(f32[3,2,2,128,128]{4,3,2,1,0:T(8,128)} %param.3) | copy-start | bytes 2359300
  9.2 18.1 %all-to-all-start = ((f32[8,2,8,1,1,16,128]{6,5,1,2,4,3,0:T(8,128)}), f32[8,2,8,1,1,16,128]{6,5,1,2,4,3,0:T(8,128)S(1)}, u32[]{:S(2)}, u32[]{:S(2)}) async-start(f32[8,2,8,1,1,16,128]{6,5,1,2,4,3,0:T(8,128)} %fusion.15), calls=%async_computation | async-start | bytes 2097152 | tf_op jit(solution)/shard_map/all_to_all | solution.py:30
  32.8 30.8 %all-to-all-start.1 = ((f32[2,8,1,1,128,128]{5,0,1,3,2,4:T(2,128)}), f32[2,8,1,1,128,128]{5,0,1,3,2,4:T(2,128)S(1)}, u32[]{:S(2)}, u32[]{:S(2)}) async-start(f32[2,8,1,1,128,128]{5,0,1,3,2,4:T(2,128)} %copy.10), calls=%async_computation.1 | async-start | bytes 2097152 | tf_op jit(solution)/shard_map/all_to_all | solution.py:38
